TPU v7x, 32 devices: a whole 2x2x4 slice. The times are simulated.
32 devices in a mesh: band: 16 (over z, y, core), pw: 2 (over x).
Axes of the slice: x: 2, y: 2, z: 4, core: 2. Of those that a mesh axis runs over, the one named last changes fastest.
Arguments:
- mel: bfloat16 [32, 256, 32768], P('band', None, 'pw'), may hold values from -6 to 6
- pole_amp: bfloat16 [32768, 256], P('pw', 'band'), may hold values from 0.19921875 to 5
- pole_freq: bfloat16 [32768, 256], P('pw', 'band'), may hold values from 0.5 to 4
- band_energy: float32 [32], P('band'), may hold values from -3 to 3
- occupation: int32 [32], P('band'), may hold values from 0 to 1
- column_map: int32 [256], replicated, may hold values from 0 to 32767
- energies: float32 [2], replicated, may hold values from -2 to 2
Outputs:
- sigma: float32 [2, 256, 256], P(None, 'pw')
All inputs are finite; a program needn't handle non-finite values.
Results may differ from a plain program's by a relative error of at most 0.0055.
Values may be sent and summed in bfloat16 or wider, within the bound.
No kernel may reach another device: no remote copies, remote signals or barrier semaphores. Data moves between devices by JAX's collectives and lax.ppermute only.
A program may use at most 64 MiB of HBM per device.

v0:
```python
import functools
import math

import jax
import jax.numpy as jnp
from jax import lax
from jax.experimental import pallas as pl
from jax.experimental.pallas import tpu as pltpu
from jax.sharding import PartitionSpec as P


broadening = 0.4
LANES = 128
VM = pltpu.VMEM


CHUNKS = 4

contract_minor = (((1,), (1,)), ((), ()))


def swap(value, axis, size, mask):
    return lax.ppermute(value, axis, [(i, i ^ mask) for i in range(size)])


def largest_block(extent, limit):
    block = extent
    while block > limit and block % (2 * LANES) == 0:
        block //= 2
    return block


def pick_kernel(sign_ref, index_ref, mel_ref, out_ref, acc_ref):
    step = pl.program_id(0)
    bands, _, width = mel_ref.shape
    columns = index_ref.shape[0]
    lane = lax.broadcasted_iota(jnp.int32, (columns, width), 1) + step * width
    hot = (lane == index_ref[...]).astype(jnp.float32).astype(jnp.bfloat16)

    @pl.when(step == 0)
    def _():
        acc_ref[...] = jnp.zeros_like(acc_ref)

    for m in range(bands):
        acc_ref[m] += lax.dot_general(
            hot, mel_ref[m], contract_minor, preferred_element_type=jnp.float32
        )

    @pl.when(step == pl.num_programs(0) - 1)
    def _():
        for m in range(bands):
            out_ref[m] = (acc_ref[m] * sign_ref[m]).astype(out_ref.dtype)


def pick(mel, index, sign):
    bands, states, rows = mel.shape
    columns = index.shape[0]
    width = largest_block(rows, 1024)
    return pl.pallas_call(
        pick_kernel,
        grid=(rows // width,),
        in_specs=[
            pl.BlockSpec(memory_space=pltpu.SMEM),
            pl.BlockSpec((columns, 1), lambda i: (0, 0)),
            pl.BlockSpec((bands, states, width), lambda i: (0, 0, i)),
        ],
        out_specs=pl.BlockSpec((bands, columns, states), lambda i: (0, 0, 0)),
        out_shape=jax.ShapeDtypeStruct((bands, columns, states), jnp.bfloat16),
        scratch_shapes=[VM((bands, columns, states), jnp.float32)],
        cost_estimate=pl.CostEstimate(
            flops=2 * bands * columns * states * rows,
            bytes_accessed=2 * mel.size,
            transcendentals=0,
        ),
        name="pick",
    )(sign, index.reshape(columns, 1), mel)


def screened_block(shift, amplitude, frequency):
    gap = [frequency + s for s in shift]
    level = [[h * h + broadening * broadening for h in gap]]
    while len(level[-1]) > 1:
        row = level[-1]
        level.append([row[i] * row[i + 1] for i in range(0, len(row) - 1, 2)] + (row[-1:] if len(row) % 2 else []))
    inverse = [amplitude / (level[-1][0] * frequency)]
    for row in reversed(level[:-1]):
        finer = []
        for i in range(len(row)):
            partner = i ^ 1
            finer.append(inverse[i // 2] * row[partner] if partner < len(row) else inverse[i // 2])
        inverse = finer
    return [h * v for h, v in zip(gap, inverse)]


def chunk_kernel(groups, energies, first, last, parts, scale, *refs):
    shift_ref, own_ref, pair_ref = refs[:3]
    items = refs[3 : 3 + groups]
    rest = list(refs[3 + groups :])
    acc_in = None if first else rest.pop(0)
    if last:
        chosen_ref, out_ref, acc_ref, work_ref = rest
    else:
        acc_ref, work_ref = rest
    step = pl.program_id(0)
    bands = own_ref.shape[0]
    width = own_ref.shape[2]
    states = own_ref.shape[1]
    height = items[0].shape[1]
    columns = height * groups

    @pl.when(step == 0)
    def _():
        acc_ref[...] = jnp.zeros_like(acc_ref) if first else acc_in[...]

    shift = [shift_ref[i] for i in range(2 * bands * energies)]
    piece = min(width, 2 * LANES)

    def fill(t, carry):
        lanes = pl.ds(pl.multiple_of(t * piece, LANES), piece)
        for g, item in enumerate(items):
            for top in range(0, height, 16):
                tall = min(16, height - top)
                amplitude = item[0, top : top + tall, lanes].astype(jnp.float32)
                frequency = item[1, top : top + tall, lanes].astype(jnp.float32)
                blocks = screened_block(shift, amplitude, frequency)
                for i, block in enumerate(blocks):
                    m, e = divmod(i, energies)
                    at = e * columns + g * height + top
                    work_ref[m, at : at + tall, lanes] = block.astype(jnp.bfloat16)
        return carry

    lax.fori_loop(0, width // piece, fill, 0)
    for m in range(2 * bands):
        elements = own_ref[m] if m < bands else pair_ref[m - bands]
        acc_ref[m] += lax.dot_general(
            elements, work_ref[m], contract_minor, preferred_element_type=jnp.float32
        )

    if last:

        @pl.when(step == pl.num_programs(0) - 1)
        def _():
            rows = states // parts
            wide = states // 2
            for e in range(energies):
                total = jnp.zeros((states, states), jnp.float32)
                for m in range(2 * bands):
                    block = acc_ref[m, :, e * columns : (e + 1) * columns]
                    upper = block.astype(jnp.bfloat16)
                    lower = (block - upper.astype(jnp.float32)).astype(jnp.bfloat16)
                    picked = chosen_ref[m]
                    total += jnp.dot(upper, picked, preferred_element_type=jnp.float32)
                    total += jnp.dot(lower, picked, preferred_element_type=jnp.float32)
                total = total * scale
                for p in range(parts):
                    for k in range(2):
                        out_ref[k, p, e * rows : (e + 1) * rows, :] = total[
                            p * rows : (p + 1) * rows, k * wide : (k + 1) * wide
                        ]


def chunk(index, count, shift, mel, pair, items, acc, chosen, parts, scale):
    bands, states, rows = mel.shape
    size = rows // count
    width = largest_block(size, 1024)
    steps = size // width
    base = index * steps
    groups = len(items)
    height = items[0].shape[1]
    columns = groups * height
    energies = shift.shape[0] // (2 * bands)
    first, last = acc is None, chosen is not None
    acc_shape = (2 * bands, states, energies * columns)
    acc_spec = pl.BlockSpec(acc_shape, lambda i: (0, 0, 0))
    mel_spec = pl.BlockSpec((bands, states, width), lambda i: (0, 0, base + i))
    operands = [shift, mel, pair, *items]
    in_specs = [pl.BlockSpec(memory_space=pltpu.SMEM), mel_spec, mel_spec]
    in_specs += [pl.BlockSpec((2, height, width), lambda i: (0, 0, i))] * groups
    if not first:
        operands.append(acc)
        in_specs.append(acc_spec)
    scratch = [VM((2 * bands, energies * columns, width), jnp.bfloat16)]
    alias = {}
    if last:
        operands.append(chosen)
        in_specs.append(pl.BlockSpec(chosen.shape, lambda i: (0, 0, 0)))
        out_shape = jax.ShapeDtypeStruct(
            (2, parts, energies * (states // parts), states // 2), jnp.float32
        )
        out_spec = pl.BlockSpec(out_shape.shape, lambda i: (0, 0, 0, 0))
        scratch = [VM(acc_shape, jnp.float32)] + scratch
    else:
        out_shape = jax.ShapeDtypeStruct(acc_shape, jnp.float32)
        out_spec = acc_spec
        if not first:
            alias = {len(operands) - 1: 0}
    flops = 2 * 2 * bands * energies * states * columns * size
    return pl.pallas_call(
        functools.partial(chunk_kernel, groups, energies, first, last, parts, scale),
        grid=(steps,),
        in_specs=in_specs,
        out_specs=out_spec,
        out_shape=out_shape,
        scratch_shapes=scratch,
        input_output_aliases=alias,
        cost_estimate=pl.CostEstimate(
            flops=4 * flops, bytes_accessed=8 * bands * states * size, transcendentals=0
        ),
        name="chunk",
    )(*operands)


def spread_kernel(count, chip_ref, a_ref, b_ref, *out_refs):
    tall = out_refs[0].shape[0]
    for d in range(count):
        at = pl.ds((chip_ref[0] ^ d) * tall, tall)
        out_refs[d][...] = a_ref[at, :] + b_ref[at, :]


def spread(chip, count, a, b):
    rows, width = a.shape
    tall = rows // count
    if tall % 8:
        both = a + b
        return [
            lax.dynamic_slice_in_dim(both, (chip ^ d) * tall, tall, 0) for d in range(count)
        ]
    return pl.pallas_call(
        functools.partial(spread_kernel, count),
        in_specs=[pl.BlockSpec(memory_space=pltpu.SMEM)] + [pl.BlockSpec(memory_space=VM)] * 2,
        out_specs=[pl.BlockSpec(memory_space=VM)] * count,
        out_shape=[jax.ShapeDtypeStruct((tall, width), jnp.float32)] * count,
        name="spread",
    )(chip.reshape(1), a, b)


def settle_kernel(count, place_ref, *refs):
    pieces, out_ref = refs[:count], refs[count]
    _, tall, wide = pieces[0].shape
    per_energy = out_ref.shape[1] // tall
    core, chip = place_ref[0], place_ref[1]
    for d in range(count):
        at = chip ^ d
        e, top = at // per_energy, (at % per_energy) * tall
        for r in range(2):
            lanes = pl.ds(pl.multiple_of((core ^ r) * wide, wide), wide)
            out_ref[e, pl.ds(pl.multiple_of(top, tall), tall), lanes] = pieces[d][r]


def settle(core, chip, pieces, energies, rows, states):
    _, tall, _ = pieces[0].shape
    count = len(pieces)
    if tall % 8:
        order = jnp.arange(count, dtype=jnp.int32) ^ chip
        cores = jnp.arange(2, dtype=jnp.int32) ^ core
        whole = jnp.stack(pieces)[order][:, cores].transpose(0, 2, 1, 3)
        return whole.reshape(energies, rows, states)
    place = jnp.stack([core, chip]).astype(jnp.int32)
    return pl.pallas_call(
        functools.partial(settle_kernel, count),
        in_specs=[pl.BlockSpec(memory_space=pltpu.SMEM)]
        + [pl.BlockSpec(memory_space=VM)] * count,
        out_specs=pl.BlockSpec(memory_space=VM),
        out_shape=jax.ShapeDtypeStruct((energies, rows, states), jnp.float32),
        name="settle",
    )(place, *pieces)


def local(bands_total, pw_total, chunks, mel, pole_amp, pole_freq, band_energy, occupation, column_map, energies):
    bands, states, rows = mel.shape
    columns = pole_amp.shape[1]
    chips = bands_total // 2
    band_at = lax.axis_index("band")
    pw_at = lax.axis_index("pw")
    core, chip = band_at % 2, band_at // 2
    energy_count = energies.shape[0]

    pair = swap(mel, "band", bands_total, 1)
    sign = (2 * occupation - 1).astype(jnp.float32)
    shift = sign[:, None] * (energies[None, :] - band_energy[:, None])
    shift = jnp.concatenate([shift, swap(shift, "band", bands_total, 1)]).reshape(-1)

    count = min(chunks, rows // LANES)
    size = rows // count
    amp_t, freq_t = pole_amp.T, pole_freq.T
    slots = []
    for c in range(count):
        window = slice(c * size, (c + 1) * size)
        slots.append({0: jnp.stack([amp_t[:, window], freq_t[:, window]])})
    tops = [1 << b for b in reversed(range(chips.bit_length() - 1))]
    for c in range(count):
        have = slots[c]
        for top in tops:
            for s in list(have):
                if c == count - 1 and s == tops[0] and top == 1:
                    continue
                have[s | top] = swap(have[s], "band", bands_total, 2 * top)
        if tops[0] | 1 not in have:
            have[tops[0] | 1] = swap(have[1], "band", bands_total, 2 * tops[0])

    order = jnp.arange(chips, dtype=jnp.int32) ^ chip
    by_device = column_map.reshape(bands_total, columns)
    mine = by_device[2 * order + core].reshape(-1)
    theirs = by_device[2 * order + (1 - core)].reshape(-1)
    index = jnp.concatenate([mine, theirs]) - pw_at * rows
    picked = pick(mel, index, sign)
    for b in range(pw_total.bit_length() - 1):
        picked = picked + swap(picked, "pw", pw_total, 1 << b)
    half = picked.shape[1] // 2
    chosen = jnp.concatenate([picked[:, :half], swap(picked[:, half:], "band", bands_total, 1)])

    scale = 1.0 / math.sqrt(rows * pw_total * column_map.shape[0] * bands * bands_total)
    acc = None
    for c in range(count):
        items = [slots[c][s] for s in range(chips)]
        if columns % 16:
            items = [jnp.concatenate(items, axis=1)]
        final = chosen if c == count - 1 else None
        acc = chunk(c, count, shift, mel, pair, items, acc, final, pw_total, scale)
    partial = acc

    keep = lax.dynamic_index_in_dim(partial, core, 0, False)
    partial = keep + swap(
        lax.dynamic_index_in_dim(partial, 1 - core, 0, False), "band", bands_total, 1
    )
    parts = pw_total
    while parts > 2:
        parts //= 2
        bit = (pw_at // parts) % 2
        keep = lax.dynamic_slice_in_dim(partial, bit * parts, parts, 0)
        give = lax.dynamic_slice_in_dim(partial, (1 - bit) * parts, parts, 0)
        partial = keep + swap(give, "pw", pw_total, parts)
    if parts == 2:
        bit = pw_at % 2
        keep = lax.dynamic_index_in_dim(partial, bit, 0, False)
        got = swap(lax.dynamic_index_in_dim(partial, 1 - bit, 0, False), "pw", pw_total, 1)
    else:
        keep = partial[0]
        got = jnp.zeros_like(keep)
    pieces = spread(chip, chips, keep, got)
    total = pieces[0]
    for d in range(1, chips):
        total = total + swap(pieces[d], "band", bands_total, 2 * d)
    both = jnp.stack([total, swap(total, "band", bands_total, 1)])
    final = [both] + [swap(both, "band", bands_total, 2 * d) for d in range(1, chips)]
    return settle(core, chip, final, energy_count, states // pw_total, states)


def solution(mesh):
    bands_total, pw_total = mesh.shape["band"], mesh.shape["pw"]

    def body(*args):
        return local(bands_total, pw_total, CHUNKS, *args)

    return jax.shard_map(
        body,
        mesh=mesh,
        in_specs=(
            P("band", None, "pw"),
            P("pw", "band"),
            P("pw", "band"),
            P("band"),
            P("band"),
            P(),
            P(),
        ),
        out_specs=P(None, "pw", None),
        check_vma=False,
    )
```

profile of v0, /device:TPU:1, one launch (start us, length us, event | category | flops | bytes accessed | tf_op | source)
XLA Modules:
  0.0 193.3 jit_solution(5215946231977422947)
XLA Ops:
  1.4 3.9 %collective-permute-start.26 = (bf16[2,16,4096]{2,1,0:T(8,128)(2,1)S(1)}, bf16[2,16,4096]{2,1,0:T(8,128)(2,1)S(1)}, u32[]{:S(2)}, u32[]{:S(2)}) collective-permute-start(bf16[2,16,4096]{2,1,0:T(8,128)(2,1)S(1)} %pad_maximum_fusion.3.refs_3_), channel_id=1, source_target_pairs={{0,16},{2,18},{4,20},{6,22},{8,24},{10,26},{12,28},{14,30},{16,0},... | collective-permute-start | bytes 786440 | tf_op jit(solution)/shard_map/ppermute | solution.py:23
  13.0 16.5 %pick.1 = bf16[2,256,256]{2,1,0:T(8,128)(2,1)} custom-call(f32[2]{0:T(128)} %copy-done.32, s32[256,1]{1,0:T(8,128)} %broadcast_subtract_fusion.index_ref, bf16[2,256,16384]{2,1,0:T(8,128)(2,1)} %refs_1_.7), custom_call_target="tpu_custom_call" | custom-call | flops 4294967296 | bytes 16777216 | tf_op jit(solution)/shard_map/pick/pallas_call | solution.py:59
  32.8 11.4 %collective-permute-done.19.refs_7_ = bf16[2,16,4096]{2,1,0:T(8,128)(2,1)S(1)} collective-permute-done((bf16[2,16,4096]{2,1,0:T(8,128)(2,1)S(1)}, bf16[2,16,4096]{2,1,0:T(8,128)(2,1)S(1)}, u32[]{:S(2)}, u32[]{:S(2)}) %collective-permute-start.19) | collective-permute-done | bytes 262176 | tf_op jit(solution)/shard_map/ppermute | solution.py:23
  45.7 1.7 collective-permute-start.9
  48.1 9.7 %collective-permute-done.12.refs_7_ = bf16[2,16,4096]{2,1,0:T(8,128)(2,1)S(1)} collective-permute-done((bf16[2,16,4096]{2,1,0:T(8,128)(2,1)S(1)}, bf16[2,16,4096]{2,1,0:T(8,128)(2,1)S(1)}, u32[]{:S(2)}, u32[]{:S(2)}) %collective-permute-start.12) | collective-permute-done | bytes 262176 | tf_op jit(solution)/shard_map/ppermute | solution.py:23
  59.7 8.2 %collective-permute-done.5.refs_7_ = bf16[2,16,4096]{2,1,0:T(8,128)(2,1)S(1)} collective-permute-done((bf16[2,16,4096]{2,1,0:T(8,128)(2,1)S(1)}, bf16[2,16,4096]{2,1,0:T(8,128)(2,1)S(1)}, u32[]{:S(2)}, u32[]{:S(2)}) %collective-permute-start.5) | collective-permute-done | bytes 262176 | tf_op jit(solution)/shard_map/ppermute | solution.py:23
  74.0 1.7 collective-permute-done.25.refs_6_
  77.9 3.5 %collective-permute-done.29.refs_10_ = bf16[2,16,4096]{2,1,0:T(8,128)(2,1)} collective-permute-done((bf16[2,16,4096]{2,1,0:T(8,128)(2,1)}, bf16[2,16,4096]{2,1,0:T(8,128)(2,1)}, u32[]{:S(2)}, u32[]{:S(2)}) %collective-permute-start.29) | collective-permute-done | bytes 262176 | tf_op jit(solution)/shard_map/ppermute | solution.py:23
  82.7 10.9 %chunk.4.refs_11_ = f32[4,256,256]{2,1,0:T(8,128)} custom-call(f32[8]{0:T(128)} %reshape.79.refs_0_, bf16[2,256,16384]{2,1,0:T(8,128)(2,1)} %refs_1_.7, bf16[2,256,16384]{2,1,0:T(8,128)(2,1)} %collective-permute-done.1.refs_2_, bf16[2,16,4096]{2,1,0:T(8,128)(2,1)} %copy-done, bf16[2,16,4096]{2,1,0:T(8,128)(2,1)} %copy-done.6, ...), custom_call_target="tpu_custom_call" | custom-call | flops 8589934592 | bytes 16777216 | tf_op jit(solution)/shard_map/chunk/pallas_call | solution.py:198
  99.5 11.8 %chunk.5.refs_11_ = f32[4,256,256]{2,1,0:T(8,128)} custom-call(f32[8]{0:T(128)} %reshape.79.refs_0_, bf16[2,256,16384]{2,1,0:T(8,128)(2,1)} %refs_1_.7, bf16[2,256,16384]{2,1,0:T(8,128)(2,1)} %collective-permute-done.1.refs_2_, bf16[2,16,4096]{2,1,0:T(8,128)(2,1)} %copy-done.3, bf16[2,16,4096]{2,1,0:T(8,128)(2,1)} %copy-done.13, ...), custom_call_target="tpu_custom_call", output_to_operand_aliasing={{}: (11, {})} | custom-call | flops 8589934592 | bytes 16777216 | tf_op jit(solution)/shard_map/chunk/pallas_call | solution.py:198
  112.9 2.1 %collective-permute-done.11.refs_6_ = bf16[2,16,4096]{2,1,0:T(8,128)(2,1)S(1)} collective-permute-done((bf16[2,16,4096]{2,1,0:T(8,128)(2,1)S(1)}, bf16[2,16,4096]{2,1,0:T(8,128)(2,1)S(1)}, u32[]{:S(2)}, u32[]{:S(2)}) %collective-permute-start.11) | collective-permute-done | bytes 262176 | tf_op jit(solution)/shard_map/ppermute | solution.py:23
  115.0 5.6 %collective-permute-done.15.refs_10_ = bf16[2,16,4096]{2,1,0:T(8,128)(2,1)S(1)} collective-permute-done((bf16[2,16,4096]{2,1,0:T(8,128)(2,1)}, bf16[2,16,4096]{2,1,0:T(8,128)(2,1)S(1)}, u32[]{:S(2)}, u32[]{:S(2)}) %collective-permute-start.15) | collective-permute-done | bytes 262176 | tf_op jit(solution)/shard_map/ppermute | solution.py:23
  121.3 11.8 %chunk.6.refs_11_ = f32[4,256,256]{2,1,0:T(8,128)} custom-call(f32[8]{0:T(128)} %reshape.79.refs_0_, bf16[2,256,16384]{2,1,0:T(8,128)(2,1)} %refs_1_.7, bf16[2,256,16384]{2,1,0:T(8,128)(2,1)} %collective-permute-done.1.refs_2_, bf16[2,16,4096]{2,1,0:T(8,128)(2,1)} %copy-done.1, bf16[2,16,4096]{2,1,0:T(8,128)(2,1)} %copy-done.11, ...), custom_call_target="tpu_custom_call", output_to_operand_aliasing={{}: (11, {})} | custom-call | flops 8589934592 | bytes 16777216 | tf_op jit(solution)/shard_map/chunk/pallas_call | solution.py:198
  134.6 12.4 %chunk.7 = f32[2,2,256,128]{3,2,1,0:T(8,128)} custom-call(f32[8]{0:T(128)} %reshape.79.refs_0_, bf16[2,256,16384]{2,1,0:T(8,128)(2,1)} %refs_1_.7, bf16[2,256,16384]{2,1,0:T(8,128)(2,1)} %collective-permute-done.1.refs_2_, bf16[2,16,4096]{2,1,0:T(8,128)(2,1)} %copy-done.2, bf16[2,16,4096]{2,1,0:T(8,128)(2,1)} %copy-done.14, ...), custom_call_target="tpu_custom_call" | custom-call | flops 8589934592 | bytes 16777216 | tf_op jit(solution)/shard_map/chunk/pallas_call | solution.py:198
  148.0 2.1 %collective-permute-start.32 = (f32[2,256,128]{2,1,0:T(8,128)S(1)}, f32[2,256,128]{2,1,0:T(8,128)S(1)}, u32[]{:S(2)}, u32[]{:S(2)}) collective-permute-start(f32[2,256,128]{2,1,0:T(8,128)S(1)} %dynamic-slice_bitcast_fusion), channel_id=1, source_target_pairs={{0,2},{2,0},{4,6},{6,4},{8,10},{10,8},{12,14},{14,12},{16,18},{18,... | collective-permute-start | bytes 786440 | tf_op jit(solution)/shard_map/ppermute | solution.py:23
  154.1 3.5 %collective-permute-done.33.b_ref = f32[256,128]{1,0:T(8,128)S(1)} collective-permute-done((f32[256,128]{1,0:T(8,128)S(1)}, f32[256,128]{1,0:T(8,128)S(1)}, u32[]{:S(2)}, u32[]{:S(2)}) %collective-permute-start.33) | collective-permute-done | bytes 131104 | tf_op jit(solution)/shard_map/ppermute | solution.py:23
  162.8 2.0 %collective-permute-start.37 = (f32[32,128]{1,0:T(8,128)}, f32[32,128]{1,0:T(8,128)S(1)}, u32[]{:S(2)}, u32[]{:S(2)}) collective-permute-start(f32[32,128]{1,0:T(8,128)} %get-tuple-element.17), channel_id=1, source_target_pairs={{0,16},{2,18},{4,20},{6,22},{8,24},{10,26},{12,28},{14,30},{16,0},... | collective-permute-start | bytes 49160 | tf_op jit(solution)/shard_map/ppermute | solution.py:23
  166.3 1.8 collective-permute-start.39
  171.0 2.7 %collective-permute-done.40 = f32[32,128]{1,0:T(8,128)S(1)} collective-permute-done((f32[32,128]{1,0:T(8,128)}, f32[32,128]{1,0:T(8,128)S(1)}, u32[]{:S(2)}, u32[]{:S(2)}) %collective-permute-start.40) | collective-permute-done | bytes 16416 | tf_op jit(solution)/shard_map/ppermute | solution.py:23
  174.4 4.1 %collective-permute-start.41 = (f32[32,128]{1,0:T(8,128)S(1)}, f32[32,128]{1,0:T(8,128)S(1)}, u32[]{:S(2)}, u32[]{:S(2)}) collective-permute-start(f32[32,128]{1,0:T(8,128)S(1)} %add_add_fusion), channel_id=1, source_target_pairs={{0,2},{2,0},{4,6},{6,4},{8,10},{10,8},{12,14},{14,12},{16,18},{18,... | collective-permute-start | bytes 49160 | tf_op jit(solution)/shard_map/ppermute | solution.py:23
  179.6 2.3 %collective-permute-start.44 = (f32[2,32,128]{2,1,0:T(8,128)S(1)}, f32[2,32,128]{2,1,0:T(8,128)S(1)}, u32[]{:S(2)}, u32[]{:S(2)}) collective-permute-start(f32[2,32,128]{2,1,0:T(8,128)S(1)} %pad_maximum_fusion.5.refs_0_), channel_id=1, source_target_pairs={{0,12},{2,14},{4,8},{6,10},{8,4},{10,6},{12,0},{14,2},{16,28},{18,... | collective-permute-start | bytes 98312 | tf_op jit(solution)/shard_map/ppermute | solution.py:23
  182.2 2.2 %collective-permute-start.46 = (f32[2,32,128]{2,1,0:T(8,128)S(1)}, f32[2,32,128]{2,1,0:T(8,128)S(1)}, u32[]{:S(2)}, u32[]{:S(2)}) collective-permute-start(f32[2,32,128]{2,1,0:T(8,128)S(1)} %pad_maximum_fusion.5.refs_0_), channel_id=1, source_target_pairs={{0,20},{2,22},{4,16},{6,18},{8,28},{10,30},{12,24},{14,26},{16,4},... | collective-permute-start | bytes 98312 | tf_op jit(solution)/shard_map/ppermute | solution.py:23
  185.5 3.0 %collective-permute-start.48 = (f32[2,32,128]{2,1,0:T(8,128)S(1)}, f32[2,32,128]{2,1,0:T(8,128)S(1)}, u32[]{:S(2)}, u32[]{:S(2)}) collective-permute-start(f32[2,32,128]{2,1,0:T(8,128)S(1)} %pad_maximum_fusion.5.refs_0_), channel_id=1, source_target_pairs={{0,28},{2,30},{4,24},{6,26},{8,20},{10,22},{12,16},{14,18},{16,12}... | collective-permute-start | bytes 98312 | tf_op jit(solution)/shard_map/ppermute | solution.py:23
  189.2 1.8 collective-permute-done.48.refs_7_
  (176 shorter events, 56.3 us)
Async XLA Ops:
  0.0 81.4 %collective-permute-start.1 = (bf16[2,256,16384]{2,1,0:T(8,128)(2,1)}, bf16[2,256,16384]{2,1,0:T(8,128)(2,1)}, u32[]{:S(2)}, u32[]{:S(2)}) collective-permute-start(bf16[2,256,16384]{2,1,0:T(8,128)(2,1)} %refs_1_.7), channel_id=1, source_target_pairs={{0,2},{2,0},{4,6},{6,4},{8,10},{10,8},{12,14},{14,12},{16,18},{18,... | collective-permute-start | bytes 50331656 | tf_op jit(solution)/shard_map/ppermute | solution.py:23
  1.4 28.1 %collective-permute-start.26 = (bf16[2,16,4096]{2,1,0:T(8,128)(2,1)S(1)}, bf16[2,16,4096]{2,1,0:T(8,128)(2,1)S(1)}, u32[]{:S(2)}, u32[]{:S(2)}) collective-permute-start(bf16[2,16,4096]{2,1,0:T(8,128)(2,1)S(1)} %pad_maximum_fusion.3.refs_3_), channel_id=1, source_target_pairs={{0,16},{2,18},{4,20},{6,22},{8,24},{10,26},{12,28},{14,30},{16,0},... | collective-permute-start | bytes 786440 | tf_op jit(solution)/shard_map/ppermute | solution.py:23
  5.3 25.6 %collective-permute-start.24 = (bf16[2,16,4096]{2,1,0:T(8,128)(2,1)S(1)}, bf16[2,16,4096]{2,1,0:T(8,128)(2,1)S(1)}, u32[]{:S(2)}, u32[]{:S(2)}) collective-permute-start(bf16[2,16,4096]{2,1,0:T(8,128)(2,1)S(1)} %pad_maximum_fusion.3.refs_3_), channel_id=1, source_target_pairs={{0,8},{2,10},{4,12},{6,14},{8,0},{10,2},{12,4},{14,6},{16,24},{18,... | collective-permute-start | bytes 786440 | tf_op jit(solution)/shard_map/ppermute | solution.py:23
  6.6 25.0 %collective-permute-start.23 = (bf16[2,16,4096]{2,1,0:T(8,128)(2,1)S(1)}, bf16[2,16,4096]{2,1,0:T(8,128)(2,1)S(1)}, u32[]{:S(2)}, u32[]{:S(2)}) collective-permute-start(bf16[2,16,4096]{2,1,0:T(8,128)(2,1)S(1)} %pad_maximum_fusion.3.refs_3_), channel_id=1, source_target_pairs={{0,4},{2,6},{4,0},{6,2},{8,12},{10,14},{12,8},{14,10},{16,20},{18,... | collective-permute-start | bytes 786440 | tf_op jit(solution)/shard_map/ppermute | solution.py:23
  9.2 20.3 %collective-permute-start = (f32[2,2]{1,0:T(2,128)S(1)}, f32[2,2]{1,0:T(2,128)S(1)}, u32[]{:S(2)}, u32[]{:S(2)}) collective-permute-start(f32[2,2]{1,0:T(2,128)S(1)} %subtract_multiply_fusion), channel_id=1, source_target_pairs={{0,2},{2,0},{4,6},{6,4},{8,10},{10,8},{12,14},{14,12},{16,18},{18,... | collective-permute-start | bytes 56 | tf_op jit(solution)/shard_map/ppermute | solution.py:23
  29.5 14.7 %collective-permute-start.19 = (bf16[2,16,4096]{2,1,0:T(8,128)(2,1)S(1)}, bf16[2,16,4096]{2,1,0:T(8,128)(2,1)S(1)}, u32[]{:S(2)}, u32[]{:S(2)}) collective-permute-start(bf16[2,16,4096]{2,1,0:T(8,128)(2,1)S(1)} %pad_maximum_fusion.2.refs_3_), channel_id=1, source_target_pairs={{0,16},{2,18},{4,20},{6,22},{8,24},{10,26},{12,28},{14,30},{16,0},... | collective-permute-start | bytes 786440 | tf_op jit(solution)/shard_map/ppermute | solution.py:23
  29.6 14.7 %collective-permute-start.30 = (bf16[2,256,256]{2,1,0:T(8,128)(2,1)}, bf16[2,256,256]{2,1,0:T(8,128)(2,1)S(1)}, u32[]{:S(2)}, u32[]{:S(2)}) collective-permute-start(bf16[2,256,256]{2,1,0:T(8,128)(2,1)} %pick.1), channel_id=1, source_target_pairs={{0,1},{1,0},{2,3},{3,2},{4,5},{5,4},{6,7},{7,6},{8,9},{9,8},{10,11... | collective-permute-start | bytes 786440 | tf_op jit(solution)/shard_map/ppermute | solution.py:23
  30.9 14.8 %collective-permute-start.17 = (bf16[2,16,4096]{2,1,0:T(8,128)(2,1)S(1)}, bf16[2,16,4096]{2,1,0:T(8,128)(2,1)S(1)}, u32[]{:S(2)}, u32[]{:S(2)}) collective-permute-start(bf16[2,16,4096]{2,1,0:T(8,128)(2,1)S(1)} %pad_maximum_fusion.2.refs_3_), channel_id=1, source_target_pairs={{0,8},{2,10},{4,12},{6,14},{8,0},{10,2},{12,4},{14,6},{16,24},{18,... | collective-permute-start | bytes 786440 | tf_op jit(solution)/shard_map/ppermute | solution.py:23
  31.6 15.8 %collective-permute-start.16 = (bf16[2,16,4096]{2,1,0:T(8,128)(2,1)S(1)}, bf16[2,16,4096]{2,1,0:T(8,128)(2,1)S(1)}, u32[]{:S(2)}, u32[]{:S(2)}) collective-permute-start(bf16[2,16,4096]{2,1,0:T(8,128)(2,1)S(1)} %pad_maximum_fusion.2.refs_3_), channel_id=1, source_target_pairs={{0,4},{2,6},{4,0},{6,2},{8,12},{10,14},{12,8},{14,10},{16,20},{18,... | collective-permute-start | bytes 786440 | tf_op jit(solution)/shard_map/ppermute | solution.py:23
  47.4 20.5 %collective-permute-start.5 = (bf16[2,16,4096]{2,1,0:T(8,128)(2,1)S(1)}, bf16[2,16,4096]{2,1,0:T(8,128)(2,1)S(1)}, u32[]{:S(2)}, u32[]{:S(2)}) collective-permute-start(bf16[2,16,4096]{2,1,0:T(8,128)(2,1)S(1)} %pad_maximum_fusion.refs_3_), channel_id=1, source_target_pairs={{0,16},{2,18},{4,20},{6,22},{8,24},{10,26},{12,28},{14,30},{16,0},... | collective-permute-start | bytes 786440 | tf_op jit(solution)/shard_map/ppermute | solution.py:23
  58.7 15.2 %collective-permute-start.27 = (bf16[2,16,4096]{2,1,0:T(8,128)(2,1)S(1)}, bf16[2,16,4096]{2,1,0:T(8,128)(2,1)}, u32[]{:S(2)}, u32[]{:S(2)}) collective-permute-start(bf16[2,16,4096]{2,1,0:T(8,128)(2,1)S(1)} %collective-permute-done.26.refs_7_), channel_id=1, source_target_pairs={{0,4},{2,6},{4,0},{6,2},{8,12},{10,14},{12,8},{14,10},{16,20},{18,... | collective-permute-start | bytes 786440 | tf_op jit(solution)/shard_map/ppermute | solution.py:23
  74.0 19.7 %collective-permute-start.3 = (bf16[2,16,4096]{2,1,0:T(8,128)(2,1)S(1)}, bf16[2,16,4096]{2,1,0:T(8,128)(2,1)}, u32[]{:S(2)}, u32[]{:S(2)}) collective-permute-start(bf16[2,16,4096]{2,1,0:T(8,128)(2,1)S(1)} %pad_maximum_fusion.refs_3_), channel_id=1, source_target_pairs={{0,8},{2,10},{4,12},{6,14},{8,0},{10,2},{12,4},{14,6},{16,24},{18,... | collective-permute-start | bytes 786440 | tf_op jit(solution)/shard_map/ppermute | solution.py:23
  75.7 18.2 %collective-permute-start.20 = (bf16[2,16,4096]{2,1,0:T(8,128)(2,1)S(1)}, bf16[2,16,4096]{2,1,0:T(8,128)(2,1)}, u32[]{:S(2)}, u32[]{:S(2)}) collective-permute-start(bf16[2,16,4096]{2,1,0:T(8,128)(2,1)S(1)} %collective-permute-done.19.refs_7_), channel_id=1, source_target_pairs={{0,4},{2,6},{4,0},{6,2},{8,12},{10,14},{12,8},{14,10},{16,20},{18,... | collective-permute-start | bytes 786440 | tf_op jit(solution)/shard_map/ppermute | solution.py:23
  77.0 18.2 %collective-permute-start.18 = (bf16[2,16,4096]{2,1,0:T(8,128)(2,1)S(1)}, bf16[2,16,4096]{2,1,0:T(8,128)(2,1)}, u32[]{:S(2)}, u32[]{:S(2)}) collective-permute-start(bf16[2,16,4096]{2,1,0:T(8,128)(2,1)S(1)} %collective-permute-done.17.refs_5_), channel_id=1, source_target_pairs={{0,4},{2,6},{4,0},{6,2},{8,12},{10,14},{12,8},{14,10},{16,20},{18,... | collective-permute-start | bytes 786440 | tf_op jit(solution)/shard_map/ppermute | solution.py:23
  81.4 14.0 %collective-permute-start.14 = (bf16[2,16,4096]{2,1,0:T(8,128)(2,1)S(1)}, bf16[2,16,4096]{2,1,0:T(8,128)(2,1)}, u32[]{:S(2)}, u32[]{:S(2)}) collective-permute-start(bf16[2,16,4096]{2,1,0:T(8,128)(2,1)S(1)} %collective-permute-done.12.refs_7_), channel_id=1, source_target_pairs={{0,8},{2,10},{4,12},{6,14},{8,0},{10,2},{12,4},{14,6},{16,24},{18,... | collective-permute-start | bytes 786440 | tf_op jit(solution)/shard_map/ppermute | solution.py:23
  81.4 16.8 %collective-permute-start.22 = (bf16[2,16,4096]{2,1,0:T(8,128)(2,1)}, bf16[2,16,4096]{2,1,0:T(8,128)(2,1)}, u32[]{:S(2)}, u32[]{:S(2)}) collective-permute-start(bf16[2,16,4096]{2,1,0:T(8,128)(2,1)} %collective-permute-done.21.refs_9_), channel_id=1, source_target_pairs={{0,4},{2,6},{4,0},{6,2},{8,12},{10,14},{12,8},{14,10},{16,20},{18,... | collective-permute-start | bytes 786440 | tf_op jit(solution)/shard_map/ppermute | solution.py:23
  93.7 17.6 %collective-permute-start.2 = (bf16[2,16,4096]{2,1,0:T(8,128)(2,1)S(1)}, bf16[2,16,4096]{2,1,0:T(8,128)(2,1)S(1)}, u32[]{:S(2)}, u32[]{:S(2)}) collective-permute-start(bf16[2,16,4096]{2,1,0:T(8,128)(2,1)S(1)} %pad_maximum_fusion.refs_3_), channel_id=1, source_target_pairs={{0,4},{2,6},{4,0},{6,2},{8,12},{10,14},{12,8},{14,10},{16,20},{18,... | collective-permute-start | bytes 786440 | tf_op jit(solution)/shard_map/ppermute | solution.py:23
  93.9 17.6 %collective-permute-start.13 = (bf16[2,16,4096]{2,1,0:T(8,128)(2,1)S(1)}, bf16[2,16,4096]{2,1,0:T(8,128)(2,1)S(1)}, u32[]{:S(2)}, u32[]{:S(2)}) collective-permute-start(bf16[2,16,4096]{2,1,0:T(8,128)(2,1)S(1)} %collective-permute-done.12.refs_7_), channel_id=1, source_target_pairs={{0,4},{2,6},{4,0},{6,2},{8,12},{10,14},{12,8},{14,10},{16,20},{18,... | collective-permute-start | bytes 786440 | tf_op jit(solution)/shard_map/ppermute | solution.py:23
  95.2 19.8 %collective-permute-start.11 = (bf16[2,16,4096]{2,1,0:T(8,128)(2,1)S(1)}, bf16[2,16,4096]{2,1,0:T(8,128)(2,1)S(1)}, u32[]{:S(2)}, u32[]{:S(2)}) collective-permute-start(bf16[2,16,4096]{2,1,0:T(8,128)(2,1)S(1)} %collective-permute-done.10.refs_5_), channel_id=1, source_target_pairs={{0,4},{2,6},{4,0},{6,2},{8,12},{10,14},{12,8},{14,10},{16,20},{18,... | collective-permute-start | bytes 786440 | tf_op jit(solution)/shard_map/ppermute | solution.py:23
  95.4 16.1 %collective-permute-start.7 = (bf16[2,16,4096]{2,1,0:T(8,128)(2,1)S(1)}, bf16[2,16,4096]{2,1,0:T(8,128)(2,1)S(1)}, u32[]{:S(2)}, u32[]{:S(2)}) collective-permute-start(bf16[2,16,4096]{2,1,0:T(8,128)(2,1)S(1)} %collective-permute-done.5.refs_7_), channel_id=1, source_target_pairs={{0,8},{2,10},{4,12},{6,14},{8,0},{10,2},{12,4},{14,6},{16,24},{18,... | collective-permute-start | bytes 786440 | tf_op jit(solution)/shard_map/ppermute | solution.py:23
  98.2 22.4 %collective-permute-start.15 = (bf16[2,16,4096]{2,1,0:T(8,128)(2,1)}, bf16[2,16,4096]{2,1,0:T(8,128)(2,1)S(1)}, u32[]{:S(2)}, u32[]{:S(2)}) collective-permute-start(bf16[2,16,4096]{2,1,0:T(8,128)(2,1)} %collective-permute-done.14.refs_9_), channel_id=1, source_target_pairs={{0,4},{2,6},{4,0},{6,2},{8,12},{10,14},{12,8},{14,10},{16,20},{18,... | collective-permute-start | bytes 786440 | tf_op jit(solution)/shard_map/ppermute | solution.py:23
  111.3 21.8 %collective-permute-start.4 = (bf16[2,16,4096]{2,1,0:T(8,128)(2,1)}, bf16[2,16,4096]{2,1,0:T(8,128)(2,1)S(1)}, u32[]{:S(2)}, u32[]{:S(2)}) collective-permute-start(bf16[2,16,4096]{2,1,0:T(8,128)(2,1)} %collective-permute-done.3.refs_5_), channel_id=1, source_target_pairs={{0,4},{2,6},{4,0},{6,2},{8,12},{10,14},{12,8},{14,10},{16,20},{18,... | collective-permute-start | bytes 786440 | tf_op jit(solution)/shard_map/ppermute | solution.py:23
  111.5 21.6 %collective-permute-start.6 = (bf16[2,16,4096]{2,1,0:T(8,128)(2,1)S(1)}, bf16[2,16,4096]{2,1,0:T(8,128)(2,1)S(1)}, u32[]{:S(2)}, u32[]{:S(2)}) collective-permute-start(bf16[2,16,4096]{2,1,0:T(8,128)(2,1)S(1)} %collective-permute-done.2.refs_4_), channel_id=1, source_target_pairs={{0,16},{2,18},{4,20},{6,22},{8,24},{10,26},{12,28},{14,30},{16,0},... | collective-permute-start | bytes 786440 | tf_op jit(solution)/shard_map/ppermute | solution.py:23
  111.6 21.6 %collective-permute-start.8 = (bf16[2,16,4096]{2,1,0:T(8,128)(2,1)S(1)}, bf16[2,16,4096]{2,1,0:T(8,128)(2,1)S(1)}, u32[]{:S(2)}, u32[]{:S(2)}) collective-permute-start(bf16[2,16,4096]{2,1,0:T(8,128)(2,1)S(1)} %collective-permute-done.7.refs_9_), channel_id=1, source_target_pairs={{0,4},{2,6},{4,0},{6,2},{8,12},{10,14},{12,8},{14,10},{16,20},{18,... | collective-permute-start | bytes 786440 | tf_op jit(solution)/shard_map/ppermute | solution.py:23
  (58 other events, 976.2 us)
where the time goes:
time: 197 us; the launch traced here: 193 us
  Pallas kernels  66.7 us (34%)
  waiting for transfers between devices  56.5 us (29%)
  starting transfers between devices  53.1 us (27%)
  local copies, waits for them, and re-layouts  9.36 us (5%)
  other arithmetic  7.31 us (4%)
    ppermute x49, waiting for transfers between devices, swap(): return lax.ppermute(value, axis, [(i, i ^ mask) for i in range(size)])  56.5 us
    ppermute x49, starting transfers between devices, swap(): return lax.ppermute(value, axis, [(i, i ^ mask) for i in range(size)])  53.1 us
    pallas_call x4, Pallas kernels, chunk(): pl.pallas_call(functools.partial(chunk_kernel, groups, energies, first, l...  46.9 us
    pallas_call x1, Pallas kernels, pick(): pl.pallas_call(pick_kernel, grid=(rows // width,), in_specs=[pl.BlockSpec...  16.5 us
  transfers between devices with their start and end apart: 49, of which 16 were waited for; matrix products, arithmetic and copies ran while one was open for 5% of the time, Pallas kernels for 26%

commit v1 on v0

v1 whole, which is shorter than its diff:
```python
import functools
import math

import jax
import jax.numpy as jnp
from jax import lax
from jax.experimental import pallas as pl
from jax.experimental.pallas import tpu as pltpu
from jax.sharding import PartitionSpec as P


broadening = 0.4
LANES = 128
VM = pltpu.VMEM


CHUNKS = 4

contract_minor = (((1,), (1,)), ((), ()))


def swap(value, axis, size, mask):
    return lax.ppermute(value, axis, [(i, i ^ mask) for i in range(size)])


def largest_block(extent, limit):
    block = extent
    while block > limit and block % (2 * LANES) == 0:
        block //= 2
    return block


def pick_kernel(height, place_ref, occupation_ref, map_ref, mel_ref, mine_ref, theirs_ref, index_ref, acc_ref):
    step = pl.program_id(0)
    bands, _, width = mel_ref.shape
    columns = map_ref.shape[0]
    chips = columns // (2 * height)

    @pl.when(step == 0)
    def _():
        acc_ref[...] = jnp.zeros_like(acc_ref)
        for other in range(2):
            for d in range(chips):
                device = 2 * (place_ref[1] ^ d) + (place_ref[0] ^ other)
                at = (other * chips + d) * height
                source = pl.ds(pl.multiple_of(device * height, height), height)
                index_ref[at : at + height, :] = map_ref[source, :] - place_ref[2]

    piece = min(width, 2 * LANES)
    index = index_ref[...] - step * width
    lane = lax.broadcasted_iota(jnp.int32, (columns, piece), 1)
    for low in range(0, width, piece):
        hot = (lane == index - low).astype(jnp.float32).astype(jnp.bfloat16)
        for m in range(bands):
            acc_ref[m] += lax.dot_general(
                hot,
                mel_ref[m, :, low : low + piece],
                contract_minor,
                preferred_element_type=jnp.float32,
            )

    @pl.when(step == pl.num_programs(0) - 1)
    def _():
        half = columns // 2
        for m in range(bands):
            sign = (2 * occupation_ref[m] - 1).astype(jnp.float32)
            signed = (acc_ref[m] * sign).astype(jnp.bfloat16)
            mine_ref[m] = signed[:half]
            theirs_ref[m] = signed[half:]


def pick(place, occupation, column_map, mel, devices):
    bands, states, rows = mel.shape
    columns = column_map.shape[0]
    width = largest_block(rows, 1024)
    out = jax.ShapeDtypeStruct((bands, columns // 2, states), jnp.bfloat16)
    out_spec = pl.BlockSpec(out.shape, lambda i: (0, 0, 0))
    height = columns // devices
    column_map = column_map.reshape(columns, 1)
    if height % 8:
        slot = jnp.arange(devices, dtype=jnp.int32)
        device = 2 * ((slot % (devices // 2)) ^ place[1]) + (slot // (devices // 2) ^ place[0])
        column_map = column_map.reshape(devices, height)[device].reshape(columns, 1)
        place = jnp.stack([jnp.zeros_like(place[0]), jnp.zeros_like(place[0]), place[2]])
        height = columns // 2
    return pl.pallas_call(
        functools.partial(pick_kernel, height),
        grid=(rows // width,),
        in_specs=[
            pl.BlockSpec(memory_space=pltpu.SMEM),
            pl.BlockSpec(memory_space=pltpu.SMEM),
            pl.BlockSpec((columns, 1), lambda i: (0, 0)),
            pl.BlockSpec((bands, states, width), lambda i: (0, 0, i)),
        ],
        out_specs=[out_spec, out_spec],
        out_shape=[out, out],
        scratch_shapes=[VM((columns, 1), jnp.int32), VM((bands, columns, states), jnp.float32)],
        cost_estimate=pl.CostEstimate(
            flops=2 * bands * columns * states * rows,
            bytes_accessed=2 * mel.size,
            transcendentals=0,
        ),
        name="pick",
    )(place, occupation, column_map, mel)


def screened_block(shift, amplitude, frequency):
    gap = [frequency + s for s in shift]
    level = [[h * h + broadening * broadening for h in gap]]
    while len(level[-1]) > 1:
        row = level[-1]
        level.append([row[i] * row[i + 1] for i in range(0, len(row) - 1, 2)] + (row[-1:] if len(row) % 2 else []))
    inverse = [amplitude / (level[-1][0] * frequency)]
    for row in reversed(level[:-1]):
        finer = []
        for i in range(len(row)):
            partner = i ^ 1
            finer.append(inverse[i // 2] * row[partner] if partner < len(row) else inverse[i // 2])
        inverse = finer
    return [h * v for h, v in zip(gap, inverse)]


def chunk_kernel(groups, energies, first, last, parts, scale, *refs):
    own_shift, pair_shift, own_ref, pair_ref = refs[:4]
    items = refs[4 : 4 + groups]
    rest = list(refs[4 + groups :])
    acc_in = None if first else rest.pop(0)
    work_ref = rest.pop()
    if last:
        acc_ref = rest.pop()
        give_ref, keep_ref = rest.pop(), rest.pop()
        place_ref, *chosen = rest
    else:
        (acc_ref,) = rest
    step = pl.program_id(0)
    bands, states, width = own_ref.shape
    height = items[0].shape[1]
    columns = height * groups

    @pl.when(step == 0)
    def _():
        acc_ref[...] = jnp.zeros_like(acc_ref) if first else acc_in[...]

    shift = [ref[m, e] for ref in (own_shift, pair_shift) for m in range(bands) for e in range(energies)]
    piece = min(width, 2 * LANES)
    span = min(width, 4 * LANES)
    for low in range(0, width, span):
        for left in range(low, low + span, piece):
            lanes = slice(left, left + piece)
            for g, item in enumerate(items):
                for top in range(0, height, 16):
                    tall = min(16, height - top)
                    amplitude = item[0, top : top + tall, lanes].astype(jnp.float32)
                    frequency = item[1, top : top + tall, lanes].astype(jnp.float32)
                    blocks = screened_block(shift, amplitude, frequency)
                    for i, block in enumerate(blocks):
                        m, e = divmod(i, energies)
                        at = e * columns + g * height + top
                        work_ref[m, at : at + tall, lanes] = block.astype(jnp.bfloat16)
        for m in range(2 * bands):
            elements = own_ref if m < bands else pair_ref
            acc_ref[m] += lax.dot_general(
                elements[m % bands, :, low : low + span],
                work_ref[m, :, low : low + span],
                contract_minor,
                preferred_element_type=jnp.float32,
            )

    if last:

        @pl.when(step == pl.num_programs(0) - 1)
        def _():
            rows = states // parts
            wide = states // 2
            half = len(chosen) // 2
            picked = []
            for m in range(2 * bands):
                group = chosen[:half] if m < bands else chosen[half:]
                value = group[0][m % bands]
                for more in group[1:]:
                    value = value + more[m % bands]
                picked.append(value)
            for e in range(energies):
                total = jnp.zeros((states, states), jnp.float32)
                for m in range(2 * bands):
                    block = acc_ref[m, :, e * columns : (e + 1) * columns]
                    upper = block.astype(jnp.bfloat16)
                    lower = (block - upper.astype(jnp.float32)).astype(jnp.bfloat16)
                    total += jnp.dot(upper, picked[m], preferred_element_type=jnp.float32)
                    total += jnp.dot(lower, picked[m], preferred_element_type=jnp.float32)
                total = total * scale
                for core in range(2):

                    @pl.when(place_ref[0] == core)
                    def _():
                        for p in range(parts):
                            block = total[p * rows : (p + 1) * rows]
                            at = slice(e * rows, (e + 1) * rows)
                            other = 1 - core
                            keep_ref[p, at, :] = block[:, core * wide : (core + 1) * wide]
                            give_ref[p, at, :] = block[:, other * wide : (other + 1) * wide]


def chunk(index, count, shifts, mel, pair, items, acc, place, chosen, parts, scale):
    bands, states, rows = mel.shape
    size = rows // count
    width = largest_block(size, 1024)
    steps = size // width
    base = index * steps
    groups = len(items)
    height = items[0].shape[1]
    columns = groups * height
    energies = shifts[0].shape[1]
    first, last = acc is None, chosen is not None
    acc_shape = (2 * bands, states, energies * columns)
    acc_spec = pl.BlockSpec(acc_shape, lambda i: (0, 0, 0))
    mel_spec = pl.BlockSpec((bands, states, width), lambda i: (0, 0, base + i))
    smem = pl.BlockSpec(memory_space=pltpu.SMEM)
    operands = [*shifts, mel, pair, *items]
    in_specs = [smem, smem, mel_spec, mel_spec]
    in_specs += [pl.BlockSpec((2, height, width), lambda i: (0, 0, i))] * groups
    if not first:
        operands.append(acc)
        in_specs.append(acc_spec)
    scratch = [VM((2 * bands, energies * columns, width), jnp.bfloat16)]
    alias = {}
    if last:
        operands += [place, *chosen]
        in_specs += [smem] + [pl.BlockSpec(c.shape, lambda i: (0, 0, 0)) for c in chosen]
        half = jax.ShapeDtypeStruct((parts, energies * (states // parts), states // 2), jnp.float32)
        out_shape = [half, half]
        out_spec = [pl.BlockSpec(half.shape, lambda i: (0, 0, 0))] * 2
        scratch = [VM(acc_shape, jnp.float32)] + scratch
    else:
        out_shape = jax.ShapeDtypeStruct(acc_shape, jnp.float32)
        out_spec = acc_spec
        if not first:
            alias = {len(operands) - 1: 0}
    flops = 2 * 2 * bands * energies * states * columns * size
    return pl.pallas_call(
        functools.partial(chunk_kernel, groups, energies, first, last, parts, scale),
        grid=(steps,),
        in_specs=in_specs,
        out_specs=out_spec,
        out_shape=out_shape,
        scratch_shapes=scratch,
        input_output_aliases=alias,
        cost_estimate=pl.CostEstimate(
            flops=4 * flops, bytes_accessed=8 * bands * states * size, transcendentals=0
        ),
        name="chunk",
    )(*operands)


def part_kernel(which, count, place_ref, a_ref, b_ref, *out_refs):
    tall = out_refs[0].shape[0]
    for d in range(count):
        if len(a_ref.shape) == 3:
            own = place_ref[which] ^ d
            out_refs[d][...] = a_ref[own] + b_ref[own]
        else:
            at = pl.ds(pl.multiple_of((place_ref[which] ^ d) * tall, tall), tall)
            out_refs[d][...] = a_ref[at, :] + b_ref[at, :]


def part(place, which, count, a, b):
    shape = a.shape[1:] if a.ndim == 3 else (a.shape[0] // count, a.shape[1])
    if shape[0] % 8:
        both = (a + b).reshape((count,) + shape)
        return [lax.dynamic_index_in_dim(both, place[which] ^ d, 0, False) for d in range(count)]
    whole = [pl.BlockSpec(x.shape, lambda n=x.ndim: (0,) * n) for x in (a, b)]
    return pl.pallas_call(
        functools.partial(part_kernel, which, count),
        in_specs=[pl.BlockSpec(memory_space=pltpu.SMEM)] + whole,
        out_specs=[pl.BlockSpec(shape, lambda: (0, 0))] * count,
        out_shape=[jax.ShapeDtypeStruct(shape, jnp.float32)] * count,
        name="part",
    )(place, a, b)


def settle_kernel(place_ref, *refs):
    pieces, out_ref = refs[:-1], refs[-1]
    near, _, tall, wide = pieces[0].shape
    per_energy = out_ref.shape[1] // tall
    for d, piece in enumerate(pieces):
        for n in range(near):
            at = (place_ref[3] ^ n) * len(pieces) + (place_ref[4] ^ d)
            e, top = at // per_energy, (at % per_energy) * tall
            for r in range(2):
                lanes = pl.ds(pl.multiple_of((place_ref[0] ^ r) * wide, wide), wide)
                out_ref[e, pl.ds(pl.multiple_of(top, tall), tall), lanes] = piece[n, r]


def settle(place, pieces, energies, rows, states):
    near, _, tall, _ = pieces[0].shape
    far = len(pieces)
    shape = (energies, rows, states)
    if tall % 8:
        order = [jnp.arange(n, dtype=jnp.int32) ^ place[i] for n, i in ((far, 4), (near, 3), (2, 0))]
        whole = jnp.stack(pieces)[order[0]][:, order[1]][:, :, order[2]]
        return whole.transpose(1, 0, 3, 2, 4).reshape(shape)
    return pl.pallas_call(
        settle_kernel,
        in_specs=[pl.BlockSpec(memory_space=pltpu.SMEM)]
        + [pl.BlockSpec(pieces[0].shape, lambda: (0, 0, 0, 0))] * far,
        out_specs=pl.BlockSpec(shape, lambda: (0, 0, 0)),
        out_shape=jax.ShapeDtypeStruct(shape, jnp.float32),
        name="settle",
    )(place, *pieces)


def local(bands_total, pw_total, chunks, mel, pole_amp, pole_freq, band_energy, occupation, column_map, energies):
    bands, states, rows = mel.shape
    columns = pole_amp.shape[1]
    chips = bands_total // 2
    band_at = lax.axis_index("band")
    pw_at = lax.axis_index("pw")
    core, chip = band_at % 2, band_at // 2
    place = jnp.stack([core, chip, pw_at * rows, chip % 2, chip // 2, pw_at % 2]).astype(jnp.int32)
    energy_count = energies.shape[0]

    pair = swap(mel, "band", bands_total, 1)
    sign = (2 * occupation - 1).astype(jnp.float32)
    shift = sign[:, None] * (energies[None, :] - band_energy[:, None])
    shifts = (shift, swap(shift, "band", bands_total, 1))

    count = min(chunks, rows // LANES)
    size = rows // count
    amp_t, freq_t = pole_amp.T, pole_freq.T
    slots = []
    for c in range(count):
        window = slice(c * size, (c + 1) * size)
        slots.append({0: jnp.stack([amp_t[:, window], freq_t[:, window]])})
    tops = [1 << b for b in reversed(range(chips.bit_length() - 1))]
    for c in range(count):
        have = slots[c]
        for top in tops:
            for s in list(have):
                if c == count - 1 and s == tops[0] and top == 1:
                    continue
                have[s | top] = swap(have[s], "band", bands_total, 2 * top)
        if tops[0] | 1 not in have:
            have[tops[0] | 1] = swap(have[1], "band", bands_total, 2 * tops[0])

    mine, theirs = pick(place, occupation, column_map, mel, bands_total)
    chosen = []
    for value in (mine, swap(theirs, "band", bands_total, 1)):
        steps = pw_total.bit_length() - 1
        for b in range(steps - 1):
            value = value + swap(value, "pw", pw_total, 1 << b)
        chosen.append(value)
        if steps:
            chosen.append(swap(value, "pw", pw_total, 1 << (steps - 1)))

    scale = 1.0 / math.sqrt(rows * pw_total * column_map.shape[0] * bands * bands_total)
    acc = None
    for c in range(count):
        items = [slots[c][s] for s in range(chips)]
        if columns % 16:
            items = [jnp.concatenate(items, axis=1)]
        final = chosen if c == count - 1 else None
        acc = chunk(c, count, shifts, mel, pair, items, acc, place, final, pw_total, scale)
    keep, give = acc

    got = swap(give, "band", bands_total, 1)
    parts = pw_total
    while parts > 2 or parts == 1:
        keep, got = keep + got, jnp.zeros_like(keep)
        if parts == 1:
            break
        parts //= 2
        bit = (pw_at // parts) % 2
        send = lax.dynamic_slice_in_dim(keep, (1 - bit) * parts, parts, 0)
        keep = lax.dynamic_slice_in_dim(keep, bit * parts, parts, 0)
        got = swap(send, "pw", pw_total, parts)
    if parts == 2:
        keep, give = part(place, 5, 2, keep, got)
        got = swap(give, "pw", pw_total, 1)
    else:
        keep, got = keep[0], got[0]
    keep, give = part(place, 3, 2, keep, got)
    pieces = part(place, 4, chips // 2, keep, swap(give, "band", bands_total, 2))
    total = pieces[0]
    for d in range(1, chips // 2):
        total = total + swap(pieces[d], "band", bands_total, 4 * d)

    total = jnp.stack([total, swap(total, "band", bands_total, 1)])
    total = jnp.stack([total, swap(total, "band", bands_total, 2)])
    final = [total] + [swap(total, "band", bands_total, 4 * d) for d in range(1, chips // 2)]
    return settle(place, final, energy_count, states // pw_total, states)


def solution(mesh):
    bands_total, pw_total = mesh.shape["band"], mesh.shape["pw"]

    def body(*args):
        return local(bands_total, pw_total, CHUNKS, *args)

    return jax.shard_map(
        body,
        mesh=mesh,
        in_specs=(
            P("band", None, "pw"),
            P("pw", "band"),
            P("pw", "band"),
            P("band"),
            P("band"),
            P(),
            P(),
        ),
        out_specs=P(None, "pw", None),
        check_vma=False,
    )
```

time: 197 us -> 190 us (0.964)
  the two profiles are of different devices: /device:TPU:1 before, /device:TPU:0 now
where the time goes in v1:
time: 190 us; the launch traced here: 189 us
  waiting for transfers between devices  69.1 us (36%)
  Pallas kernels  65 us (34%)
  starting transfers between devices  42.4 us (22%)
  local copies, waits for them, and re-layouts  9.75 us (5%)
  other arithmetic  2.24 us (1%)
    ppermute x44, waiting for transfers between devices, swap(): return lax.ppermute(value, axis, [(i, i ^ mask) for i in range(size)])  69.1 us
    pallas_call x4, Pallas kernels, chunk(): pl.pallas_call(functools.partial(chunk_kernel, groups, energies, first, l...  42.6 us
    ppermute x44, starting transfers between devices, swap(): return lax.ppermute(value, axis, [(i, i ^ mask) for i in range(size)])  42.4 us
    pallas_call x1, Pallas kernels, pick(): pl.pallas_call(functools.partial(pick_kernel, height), grid=(rows // widt...  15.7 us
    unnamed x76, local copies, waits for them, and re-layouts  6.26 us
    pallas_call x3, Pallas kernels, part(): pl.pallas_call(functools.partial(part_kernel, which, count), in_specs=[pl...  4.93 us
  transfers between devices with their start and end apart: 44, of which 20 were waited for; matrix products, arithmetic and copies ran while one was open for 3% of the time, Pallas kernels for 25%

profile of v1, /device:TPU:0, one launch (start us, length us, event | category | flops | bytes accessed | tf_op | source)
XLA Modules:
  0.0 189.0 jit_solution(6754619522191811882)
XLA Ops:
  1.9 3.6 %collective-permute-start.26 = (bf16[2,16,4096]{2,1,0:T(8,128)(2,1)S(1)}, bf16[2,16,4096]{2,1,0:T(8,128)(2,1)S(1)}, u32[]{:S(2)}, u32[]{:S(2)}) collective-permute-start(bf16[2,16,4096]{2,1,0:T(8,128)(2,1)S(1)} %pad_maximum_fusion.3.refs_4_), channel_id=1, source_target_pairs={{0,16},{2,18},{4,20},{6,22},{8,24},{10,26},{12,28},{14,30},{16,0},... | collective-permute-start | bytes 786440 | tf_op jit(solution)/shard_map/ppermute | solution.py:23
  12.2 15.7 %pick.1 = (bf16[2,128,256]{2,1,0:T(8,128)(2,1)}, bf16[2,128,256]{2,1,0:T(8,128)(2,1)}) custom-call(s32[6]{0:T(128)} %stack.81.place_ref.refs_13_, s32[2]{0:T(128)} %occupation_ref.1, s32[256,1]{1,0:T(8,128)} %copy.10.map_ref, bf16[2,256,16384]{2,1,0:T(8,128)(2,1)} %refs_2_.7), custom_call_target="tpu_custom_call" | custom-call | flops 4294967296 | bytes 16777216 | tf_op jit(solution)/shard_map/pick/pallas_call | solution.py:86
  34.7 10.8 %collective-permute-done.19.refs_8_ = bf16[2,16,4096]{2,1,0:T(8,128)(2,1)S(1)} collective-permute-done((bf16[2,16,4096]{2,1,0:T(8,128)(2,1)S(1)}, bf16[2,16,4096]{2,1,0:T(8,128)(2,1)S(1)}, u32[]{:S(2)}, u32[]{:S(2)}) %collective-permute-start.19) | collective-permute-done | bytes 262176 | tf_op jit(solution)/shard_map/ppermute | solution.py:23
  47.0 3.0 %collective-permute-start.5 = (bf16[2,16,4096]{2,1,0:T(8,128)(2,1)S(1)}, bf16[2,16,4096]{2,1,0:T(8,128)(2,1)S(1)}, u32[]{:S(2)}, u32[]{:S(2)}) collective-permute-start(bf16[2,16,4096]{2,1,0:T(8,128)(2,1)S(1)} %pad_maximum_fusion.refs_4_), channel_id=1, source_target_pairs={{0,16},{2,18},{4,20},{6,22},{8,24},{10,26},{12,28},{14,30},{16,0},... | collective-permute-start | bytes 786440 | tf_op jit(solution)/shard_map/ppermute | solution.py:23
  50.0 6.8 %collective-permute-done.12.refs_8_ = bf16[2,16,4096]{2,1,0:T(8,128)(2,1)S(1)} collective-permute-done((bf16[2,16,4096]{2,1,0:T(8,128)(2,1)S(1)}, bf16[2,16,4096]{2,1,0:T(8,128)(2,1)S(1)}, u32[]{:S(2)}, u32[]{:S(2)}) %collective-permute-start.12) | collective-permute-done | bytes 262176 | tf_op jit(solution)/shard_map/ppermute | solution.py:23
  56.8 2.5 %collective-permute-done.10.refs_6_ = bf16[2,16,4096]{2,1,0:T(8,128)(2,1)S(1)} collective-permute-done((bf16[2,16,4096]{2,1,0:T(8,128)(2,1)S(1)}, bf16[2,16,4096]{2,1,0:T(8,128)(2,1)S(1)}, u32[]{:S(2)}, u32[]{:S(2)}) %collective-permute-start.10) | collective-permute-done | bytes 262176 | tf_op jit(solution)/shard_map/ppermute | solution.py:23
  61.3 6.2 %collective-permute-done.5.refs_8_ = bf16[2,16,4096]{2,1,0:T(8,128)(2,1)S(1)} collective-permute-done((bf16[2,16,4096]{2,1,0:T(8,128)(2,1)S(1)}, bf16[2,16,4096]{2,1,0:T(8,128)(2,1)S(1)}, u32[]{:S(2)}, u32[]{:S(2)}) %collective-permute-start.5) | collective-permute-done | bytes 262176 | tf_op jit(solution)/shard_map/ppermute | solution.py:23
  67.5 3.4 %collective-permute-done.28.refs_10_ = bf16[2,16,4096]{2,1,0:T(8,128)(2,1)S(1)} collective-permute-done((bf16[2,16,4096]{2,1,0:T(8,128)(2,1)S(1)}, bf16[2,16,4096]{2,1,0:T(8,128)(2,1)S(1)}, u32[]{:S(2)}, u32[]{:S(2)}) %collective-permute-start.28) | collective-permute-done | bytes 262176 | tf_op jit(solution)/shard_map/ppermute | solution.py:23
  73.0 3.8 %collective-permute-done.21.refs_10_ = bf16[2,16,4096]{2,1,0:T(8,128)(2,1)} collective-permute-done((bf16[2,16,4096]{2,1,0:T(8,128)(2,1)S(1)}, bf16[2,16,4096]{2,1,0:T(8,128)(2,1)}, u32[]{:S(2)}, u32[]{:S(2)}) %collective-permute-start.21) | collective-permute-done | bytes 262176 | tf_op jit(solution)/shard_map/ppermute | solution.py:23
  77.4 2.7 %collective-permute-done.29.refs_11_ = bf16[2,16,4096]{2,1,0:T(8,128)(2,1)S(1)} collective-permute-done((bf16[2,16,4096]{2,1,0:T(8,128)(2,1)S(1)}, bf16[2,16,4096]{2,1,0:T(8,128)(2,1)S(1)}, u32[]{:S(2)}, u32[]{:S(2)}) %collective-permute-start.29) | collective-permute-done | bytes 262176 | tf_op jit(solution)/shard_map/ppermute | solution.py:23
  80.9 9.7 %chunk.4.refs_12_ = f32[4,256,256]{2,1,0:T(8,128)} custom-call(f32[2,2]{1,0:T(2,128)} %copy-done.36, f32[2,2]{1,0:T(2,128)} %copy-done.37, bf16[2,256,16384]{2,1,0:T(8,128)(2,1)} %refs_2_.7, bf16[2,256,16384]{2,1,0:T(8,128)(2,1)} %collective-permute-done.1.refs_3_, bf16[2,16,4096]{2,1,0:T(8,128)(2,1)} %copy-done, bf16[2,16,4096]{2,1,0:T(8,128)(2,1)} %copy-done.6, ...), custom_call_target="tpu_custom_call" | custom-call | flops 8589934592 | bytes 16777216 | tf_op jit(solution)/shard_map/chunk/pallas_call | solution.py:240
  90.6 2.1 %collective-permute-start.2 = (bf16[2,16,4096]{2,1,0:T(8,128)(2,1)S(1)}, bf16[2,16,4096]{2,1,0:T(8,128)(2,1)S(1)}, u32[]{:S(2)}, u32[]{:S(2)}) collective-permute-start(bf16[2,16,4096]{2,1,0:T(8,128)(2,1)S(1)} %pad_maximum_fusion.refs_4_), channel_id=1, source_target_pairs={{0,4},{2,6},{4,0},{6,2},{8,12},{10,14},{12,8},{14,10},{16,20},{18,... | collective-permute-start | bytes 786440 | tf_op jit(solution)/shard_map/ppermute | solution.py:23
  97.0 10.5 %chunk.5.refs_12_ = f32[4,256,256]{2,1,0:T(8,128)} custom-call(f32[2,2]{1,0:T(2,128)} %copy-done.36, f32[2,2]{1,0:T(2,128)} %copy-done.37, bf16[2,256,16384]{2,1,0:T(8,128)(2,1)} %refs_2_.7, bf16[2,256,16384]{2,1,0:T(8,128)(2,1)} %collective-permute-done.1.refs_3_, bf16[2,16,4096]{2,1,0:T(8,128)(2,1)} %copy-done.3, ...), custom_call_target="tpu_custom_call", output_to_operand_aliasing={{}: (12, {})} | custom-call | flops 8589934592 | bytes 16777216 | tf_op jit(solution)/shard_map/chunk/pallas_call | solution.py:240
  109.7 4.1 %collective-permute-done.11.refs_7_ = bf16[2,16,4096]{2,1,0:T(8,128)(2,1)S(1)} collective-permute-done((bf16[2,16,4096]{2,1,0:T(8,128)(2,1)S(1)}, bf16[2,16,4096]{2,1,0:T(8,128)(2,1)S(1)}, u32[]{:S(2)}, u32[]{:S(2)}) %collective-permute-start.11) | collective-permute-done | bytes 262176 | tf_op jit(solution)/shard_map/ppermute | solution.py:23
  115.7 3.7 %collective-permute-done.15.refs_11_ = bf16[2,16,4096]{2,1,0:T(8,128)(2,1)S(1)} collective-permute-done((bf16[2,16,4096]{2,1,0:T(8,128)(2,1)}, bf16[2,16,4096]{2,1,0:T(8,128)(2,1)S(1)}, u32[]{:S(2)}, u32[]{:S(2)}) %collective-permute-start.15) | collective-permute-done | bytes 262176 | tf_op jit(solution)/shard_map/ppermute | solution.py:23
  120.1 10.5 %chunk.6.refs_12_ = f32[4,256,256]{2,1,0:T(8,128)} custom-call(f32[2,2]{1,0:T(2,128)} %copy-done.36, f32[2,2]{1,0:T(2,128)} %copy-done.37, bf16[2,256,16384]{2,1,0:T(8,128)(2,1)} %refs_2_.7, bf16[2,256,16384]{2,1,0:T(8,128)(2,1)} %collective-permute-done.1.refs_3_, bf16[2,16,4096]{2,1,0:T(8,128)(2,1)} %copy-done.1, ...), custom_call_target="tpu_custom_call", output_to_operand_aliasing={{}: (12, {})} | custom-call | flops 8589934592 | bytes 16777216 | tf_op jit(solution)/shard_map/chunk/pallas_call | solution.py:240
  132.3 11.9 %chunk.7 = (f32[2,256,128]{2,1,0:T(8,128)}, f32[2,256,128]{2,1,0:T(8,128)}) custom-call(f32[2,2]{1,0:T(2,128)} %copy-done.36, f32[2,2]{1,0:T(2,128)} %copy-done.37, bf16[2,256,16384]{2,1,0:T(8,128)(2,1)} %refs_2_.7, bf16[2,256,16384]{2,1,0:T(8,128)(2,1)} %collective-permute-done.1.refs_3_, bf16[2,16,4096]{2,1,0:T(8,128)(2,1)} %copy-done.2, ...), custom_call_target="tpu_custom_call" | custom-call | flops 8589934592 | bytes 16777216 | tf_op jit(solution)/shard_map/chunk/pallas_call | solution.py:240
  149.9 4.3 %collective-permute-done.34.b_ref = f32[256,128]{1,0:T(8,128)S(1)} collective-permute-done((f32[256,128]{1,0:T(8,128)}, f32[256,128]{1,0:T(8,128)S(1)}, u32[]{:S(2)}, u32[]{:S(2)}) %collective-permute-start.34) | collective-permute-done | bytes 131104 | tf_op jit(solution)/shard_map/ppermute | solution.py:23
  157.8 3.2 %collective-permute-done.35.b_ref = f32[128,128]{1,0:T(8,128)S(1)} collective-permute-done((f32[128,128]{1,0:T(8,128)}, f32[128,128]{1,0:T(8,128)S(1)}, u32[]{:S(2)}, u32[]{:S(2)}) %collective-permute-start.35) | collective-permute-done | bytes 65568 | tf_op jit(solution)/shard_map/ppermute | solution.py:23
  163.1 3.7 %collective-permute-start.37 = (f32[32,128]{1,0:T(8,128)}, f32[32,128]{1,0:T(8,128)S(1)}, u32[]{:S(2)}, u32[]{:S(2)}) collective-permute-start(f32[32,128]{1,0:T(8,128)} %get-tuple-element.27), channel_id=1, source_target_pairs={{0,16},{2,18},{4,20},{6,22},{8,24},{10,26},{12,28},{14,30},{16,0},... | collective-permute-start | bytes 49160 | tf_op jit(solution)/shard_map/ppermute | solution.py:23
  168.8 3.8 %collective-permute-done.38 = f32[32,128]{1,0:T(8,128)S(1)} collective-permute-done((f32[32,128]{1,0:T(8,128)}, f32[32,128]{1,0:T(8,128)S(1)}, u32[]{:S(2)}, u32[]{:S(2)}) %collective-permute-start.38) | collective-permute-done | bytes 16416 | tf_op jit(solution)/shard_map/ppermute | solution.py:23
  175.2 3.2 %collective-permute-done.40 = f32[2,32,128]{2,1,0:T(8,128)S(1)} collective-permute-done((f32[2,32,128]{2,1,0:T(8,128)S(1)}, f32[2,32,128]{2,1,0:T(8,128)S(1)}, u32[]{:S(2)}, u32[]{:S(2)}) %collective-permute-start.40) | collective-permute-done | bytes 32800 | tf_op jit(solution)/shard_map/ppermute | solution.py:23
  179.7 3.1 %collective-permute-start.43 = (f32[2,2,32,128]{3,2,1,0:T(8,128)S(1)}, f32[2,2,32,128]{3,2,1,0:T(8,128)S(1)}, u32[]{:S(2)}, u32[]{:S(2)}) collective-permute-start(f32[2,2,32,128]{3,2,1,0:T(8,128)S(1)} %pad_maximum_fusion.4.refs_0_), channel_id=1, source_target_pairs={{0,24},{2,26},{4,28},{6,30},{8,16},{10,18},{12,20},{14,22},{16,8},... | collective-permute-start | bytes 196616 | tf_op jit(solution)/shard_map/ppermute | solution.py:23
  182.9 3.1 %collective-permute-done.42.refs_2_ = f32[2,2,32,128]{3,2,1,0:T(8,128)S(1)} collective-permute-done((f32[2,2,32,128]{3,2,1,0:T(8,128)S(1)}, f32[2,2,32,128]{3,2,1,0:T(8,128)S(1)}, u32[]{:S(2)}, u32[]{:S(2)}) %collective-permute-start.42) | collective-permute-done | bytes 65568 | tf_op jit(solution)/shard_map/ppermute | solution.py:23
  (161 shorter events, 53.2 us)
Async XLA Ops:
  0.0 80.1 %collective-permute-start.1 = (bf16[2,256,16384]{2,1,0:T(8,128)(2,1)}, bf16[2,256,16384]{2,1,0:T(8,128)(2,1)}, u32[]{:S(2)}, u32[]{:S(2)}) collective-permute-start(bf16[2,256,16384]{2,1,0:T(8,128)(2,1)} %refs_2_.7), channel_id=1, source_target_pairs={{0,2},{2,0},{4,6},{6,4},{8,10},{10,8},{12,14},{14,12},{16,18},{18,... | collective-permute-start | bytes 50331656 | tf_op jit(solution)/shard_map/ppermute | solution.py:23
  1.9 29.4 %collective-permute-start.26 = (bf16[2,16,4096]{2,1,0:T(8,128)(2,1)S(1)}, bf16[2,16,4096]{2,1,0:T(8,128)(2,1)S(1)}, u32[]{:S(2)}, u32[]{:S(2)}) collective-permute-start(bf16[2,16,4096]{2,1,0:T(8,128)(2,1)S(1)} %pad_maximum_fusion.3.refs_4_), channel_id=1, source_target_pairs={{0,16},{2,18},{4,20},{6,22},{8,24},{10,26},{12,28},{14,30},{16,0},... | collective-permute-start | bytes 786440 | tf_op jit(solution)/shard_map/ppermute | solution.py:23
  5.5 27.3 %collective-permute-start.24 = (bf16[2,16,4096]{2,1,0:T(8,128)(2,1)S(1)}, bf16[2,16,4096]{2,1,0:T(8,128)(2,1)S(1)}, u32[]{:S(2)}, u32[]{:S(2)}) collective-permute-start(bf16[2,16,4096]{2,1,0:T(8,128)(2,1)S(1)} %pad_maximum_fusion.3.refs_4_), channel_id=1, source_target_pairs={{0,8},{2,10},{4,12},{6,14},{8,0},{10,2},{12,4},{14,6},{16,24},{18,... | collective-permute-start | bytes 786440 | tf_op jit(solution)/shard_map/ppermute | solution.py:23
  7.1 27.3 %collective-permute-start.23 = (bf16[2,16,4096]{2,1,0:T(8,128)(2,1)S(1)}, bf16[2,16,4096]{2,1,0:T(8,128)(2,1)S(1)}, u32[]{:S(2)}, u32[]{:S(2)}) collective-permute-start(bf16[2,16,4096]{2,1,0:T(8,128)(2,1)S(1)} %pad_maximum_fusion.3.refs_4_), channel_id=1, source_target_pairs={{0,4},{2,6},{4,0},{6,2},{8,12},{10,14},{12,8},{14,10},{16,20},{18,... | collective-permute-start | bytes 786440 | tf_op jit(solution)/shard_map/ppermute | solution.py:23
  10.0 17.9 %collective-permute-start = (f32[2,2]{1,0:T(2,128)S(1)}, f32[2,2]{1,0:T(2,128)S(1)}, u32[]{:S(2)}, u32[]{:S(2)}) collective-permute-start(f32[2,2]{1,0:T(2,128)S(1)} %subtract_multiply_fusion.refs_0_), channel_id=1, source_target_pairs={{0,2},{2,0},{4,6},{6,4},{8,10},{10,8},{12,14},{14,12},{16,18},{18,... | collective-permute-start | bytes 56 | tf_op jit(solution)/shard_map/ppermute | solution.py:23
  29.9 15.7 %collective-permute-start.19 = (bf16[2,16,4096]{2,1,0:T(8,128)(2,1)S(1)}, bf16[2,16,4096]{2,1,0:T(8,128)(2,1)S(1)}, u32[]{:S(2)}, u32[]{:S(2)}) collective-permute-start(bf16[2,16,4096]{2,1,0:T(8,128)(2,1)S(1)} %pad_maximum_fusion.2.refs_4_), channel_id=1, source_target_pairs={{0,16},{2,18},{4,20},{6,22},{8,24},{10,26},{12,28},{14,30},{16,0},... | collective-permute-start | bytes 786440 | tf_op jit(solution)/shard_map/ppermute | solution.py:23
  31.3 14.3 %collective-permute-start.17 = (bf16[2,16,4096]{2,1,0:T(8,128)(2,1)S(1)}, bf16[2,16,4096]{2,1,0:T(8,128)(2,1)S(1)}, u32[]{:S(2)}, u32[]{:S(2)}) collective-permute-start(bf16[2,16,4096]{2,1,0:T(8,128)(2,1)S(1)} %pad_maximum_fusion.2.refs_4_), channel_id=1, source_target_pairs={{0,8},{2,10},{4,12},{6,14},{8,0},{10,2},{12,4},{14,6},{16,24},{18,... | collective-permute-start | bytes 786440 | tf_op jit(solution)/shard_map/ppermute | solution.py:23
  32.8 14.2 %collective-permute-start.16 = (bf16[2,16,4096]{2,1,0:T(8,128)(2,1)S(1)}, bf16[2,16,4096]{2,1,0:T(8,128)(2,1)S(1)}, u32[]{:S(2)}, u32[]{:S(2)}) collective-permute-start(bf16[2,16,4096]{2,1,0:T(8,128)(2,1)S(1)} %pad_maximum_fusion.2.refs_4_), channel_id=1, source_target_pairs={{0,4},{2,6},{4,0},{6,2},{8,12},{10,14},{12,8},{14,10},{16,20},{18,... | collective-permute-start | bytes 786440 | tf_op jit(solution)/shard_map/ppermute | solution.py:23
  34.4 22.5 %collective-permute-start.12 = (bf16[2,16,4096]{2,1,0:T(8,128)(2,1)S(1)}, bf16[2,16,4096]{2,1,0:T(8,128)(2,1)S(1)}, u32[]{:S(2)}, u32[]{:S(2)}) collective-permute-start(bf16[2,16,4096]{2,1,0:T(8,128)(2,1)S(1)} %pad_maximum_fusion.1.refs_4_), channel_id=1, source_target_pairs={{0,16},{2,18},{4,20},{6,22},{8,24},{10,26},{12,28},{14,30},{16,0},... | collective-permute-start | bytes 786440 | tf_op jit(solution)/shard_map/ppermute | solution.py:23
  47.0 20.5 %collective-permute-start.5 = (bf16[2,16,4096]{2,1,0:T(8,128)(2,1)S(1)}, bf16[2,16,4096]{2,1,0:T(8,128)(2,1)S(1)}, u32[]{:S(2)}, u32[]{:S(2)}) collective-permute-start(bf16[2,16,4096]{2,1,0:T(8,128)(2,1)S(1)} %pad_maximum_fusion.refs_4_), channel_id=1, source_target_pairs={{0,16},{2,18},{4,20},{6,22},{8,24},{10,26},{12,28},{14,30},{16,0},... | collective-permute-start | bytes 786440 | tf_op jit(solution)/shard_map/ppermute | solution.py:23
  70.9 19.7 %collective-permute-start.3 = (bf16[2,16,4096]{2,1,0:T(8,128)(2,1)S(1)}, bf16[2,16,4096]{2,1,0:T(8,128)(2,1)}, u32[]{:S(2)}, u32[]{:S(2)}) collective-permute-start(bf16[2,16,4096]{2,1,0:T(8,128)(2,1)S(1)} %pad_maximum_fusion.refs_4_), channel_id=1, source_target_pairs={{0,8},{2,10},{4,12},{6,14},{8,0},{10,2},{12,4},{14,6},{16,24},{18,... | collective-permute-start | bytes 786440 | tf_op jit(solution)/shard_map/ppermute | solution.py:23
  72.3 20.5 %collective-permute-start.20 = (bf16[2,16,4096]{2,1,0:T(8,128)(2,1)S(1)}, bf16[2,16,4096]{2,1,0:T(8,128)(2,1)}, u32[]{:S(2)}, u32[]{:S(2)}) collective-permute-start(bf16[2,16,4096]{2,1,0:T(8,128)(2,1)S(1)} %collective-permute-done.19.refs_8_), channel_id=1, source_target_pairs={{0,4},{2,6},{4,0},{6,2},{8,12},{10,14},{12,8},{14,10},{16,20},{18,... | collective-permute-start | bytes 786440 | tf_op jit(solution)/shard_map/ppermute | solution.py:23
  76.8 16.0 %collective-permute-start.18 = (bf16[2,16,4096]{2,1,0:T(8,128)(2,1)S(1)}, bf16[2,16,4096]{2,1,0:T(8,128)(2,1)}, u32[]{:S(2)}, u32[]{:S(2)}) collective-permute-start(bf16[2,16,4096]{2,1,0:T(8,128)(2,1)S(1)} %collective-permute-done.17.refs_6_), channel_id=1, source_target_pairs={{0,4},{2,6},{4,0},{6,2},{8,12},{10,14},{12,8},{14,10},{16,20},{18,... | collective-permute-start | bytes 786440 | tf_op jit(solution)/shard_map/ppermute | solution.py:23
  80.1 14.7 %collective-permute-start.14 = (bf16[2,16,4096]{2,1,0:T(8,128)(2,1)S(1)}, bf16[2,16,4096]{2,1,0:T(8,128)(2,1)}, u32[]{:S(2)}, u32[]{:S(2)}) collective-permute-start(bf16[2,16,4096]{2,1,0:T(8,128)(2,1)S(1)} %collective-permute-done.12.refs_8_), channel_id=1, source_target_pairs={{0,8},{2,10},{4,12},{6,14},{8,0},{10,2},{12,4},{14,6},{16,24},{18,... | collective-permute-start | bytes 786440 | tf_op jit(solution)/shard_map/ppermute | solution.py:23
  80.8 16.2 %collective-permute-start.22 = (bf16[2,16,4096]{2,1,0:T(8,128)(2,1)}, bf16[2,16,4096]{2,1,0:T(8,128)(2,1)}, u32[]{:S(2)}, u32[]{:S(2)}) collective-permute-start(bf16[2,16,4096]{2,1,0:T(8,128)(2,1)} %collective-permute-done.21.refs_10_), channel_id=1, source_target_pairs={{0,4},{2,6},{4,0},{6,2},{8,12},{10,14},{12,8},{14,10},{16,20},{18,... | collective-permute-start | bytes 786440 | tf_op jit(solution)/shard_map/ppermute | solution.py:23
  90.6 16.9 %collective-permute-start.2 = (bf16[2,16,4096]{2,1,0:T(8,128)(2,1)S(1)}, bf16[2,16,4096]{2,1,0:T(8,128)(2,1)S(1)}, u32[]{:S(2)}, u32[]{:S(2)}) collective-permute-start(bf16[2,16,4096]{2,1,0:T(8,128)(2,1)S(1)} %pad_maximum_fusion.refs_4_), channel_id=1, source_target_pairs={{0,4},{2,6},{4,0},{6,2},{8,12},{10,14},{12,8},{14,10},{16,20},{18,... | collective-permute-start | bytes 786440 | tf_op jit(solution)/shard_map/ppermute | solution.py:23
  92.7 16.4 %collective-permute-start.13 = (bf16[2,16,4096]{2,1,0:T(8,128)(2,1)S(1)}, bf16[2,16,4096]{2,1,0:T(8,128)(2,1)S(1)}, u32[]{:S(2)}, u32[]{:S(2)}) collective-permute-start(bf16[2,16,4096]{2,1,0:T(8,128)(2,1)S(1)} %collective-permute-done.12.refs_8_), channel_id=1, source_target_pairs={{0,4},{2,6},{4,0},{6,2},{8,12},{10,14},{12,8},{14,10},{16,20},{18,... | collective-permute-start | bytes 786440 | tf_op jit(solution)/shard_map/ppermute | solution.py:23
  92.8 21.0 %collective-permute-start.11 = (bf16[2,16,4096]{2,1,0:T(8,128)(2,1)S(1)}, bf16[2,16,4096]{2,1,0:T(8,128)(2,1)S(1)}, u32[]{:S(2)}, u32[]{:S(2)}) collective-permute-start(bf16[2,16,4096]{2,1,0:T(8,128)(2,1)S(1)} %collective-permute-done.10.refs_6_), channel_id=1, source_target_pairs={{0,4},{2,6},{4,0},{6,2},{8,12},{10,14},{12,8},{14,10},{16,20},{18,... | collective-permute-start | bytes 786440 | tf_op jit(solution)/shard_map/ppermute | solution.py:23
  94.8 19.0 %collective-permute-start.7 = (bf16[2,16,4096]{2,1,0:T(8,128)(2,1)S(1)}, bf16[2,16,4096]{2,1,0:T(8,128)(2,1)S(1)}, u32[]{:S(2)}, u32[]{:S(2)}) collective-permute-start(bf16[2,16,4096]{2,1,0:T(8,128)(2,1)S(1)} %collective-permute-done.5.refs_8_), channel_id=1, source_target_pairs={{0,8},{2,10},{4,12},{6,14},{8,0},{10,2},{12,4},{14,6},{16,24},{18,... | collective-permute-start | bytes 786440 | tf_op jit(solution)/shard_map/ppermute | solution.py:23
  97.0 22.4 %collective-permute-start.15 = (bf16[2,16,4096]{2,1,0:T(8,128)(2,1)}, bf16[2,16,4096]{2,1,0:T(8,128)(2,1)S(1)}, u32[]{:S(2)}, u32[]{:S(2)}) collective-permute-start(bf16[2,16,4096]{2,1,0:T(8,128)(2,1)} %collective-permute-done.14.refs_10_), channel_id=1, source_target_pairs={{0,4},{2,6},{4,0},{6,2},{8,12},{10,14},{12,8},{14,10},{16,20},{18,... | collective-permute-start | bytes 786440 | tf_op jit(solution)/shard_map/ppermute | solution.py:23
  107.6 23.1 %collective-permute-start.30 = (bf16[2,128,256]{2,1,0:T(8,128)(2,1)S(1)}, bf16[2,128,256]{2,1,0:T(8,128)(2,1)S(1)}, u32[]{:S(2)}, u32[]{:S(2)}) collective-permute-start(bf16[2,128,256]{2,1,0:T(8,128)(2,1)S(1)} %copy-done.28), channel_id=1, source_target_pairs={{0,1},{1,0},{2,3},{3,2},{4,5},{5,4},{6,7},{7,6},{8,9},{9,8},{10,11... | collective-permute-start | bytes 393224 | tf_op jit(solution)/shard_map/ppermute | solution.py:23
  109.1 21.6 %collective-permute-start.32 = (bf16[2,128,256]{2,1,0:T(8,128)(2,1)}, bf16[2,128,256]{2,1,0:T(8,128)(2,1)S(1)}, u32[]{:S(2)}, u32[]{:S(2)}) collective-permute-start(bf16[2,128,256]{2,1,0:T(8,128)(2,1)} %collective-permute-done.31.refs_16_), channel_id=1, source_target_pairs={{0,1},{1,0},{2,3},{3,2},{4,5},{5,4},{6,7},{7,6},{8,9},{9,8},{10,11... | collective-permute-start | bytes 393224 | tf_op jit(solution)/shard_map/ppermute | solution.py:23
  113.8 16.9 %collective-permute-start.4 = (bf16[2,16,4096]{2,1,0:T(8,128)(2,1)}, bf16[2,16,4096]{2,1,0:T(8,128)(2,1)S(1)}, u32[]{:S(2)}, u32[]{:S(2)}) collective-permute-start(bf16[2,16,4096]{2,1,0:T(8,128)(2,1)} %collective-permute-done.3.refs_6_), channel_id=1, source_target_pairs={{0,4},{2,6},{4,0},{6,2},{8,12},{10,14},{12,8},{14,10},{16,20},{18,... | collective-permute-start | bytes 786440 | tf_op jit(solution)/shard_map/ppermute | solution.py:23
  113.8 16.9 %collective-permute-start.6 = (bf16[2,16,4096]{2,1,0:T(8,128)(2,1)S(1)}, bf16[2,16,4096]{2,1,0:T(8,128)(2,1)S(1)}, u32[]{:S(2)}, u32[]{:S(2)}) collective-permute-start(bf16[2,16,4096]{2,1,0:T(8,128)(2,1)S(1)} %collective-permute-done.2.refs_5_), channel_id=1, source_target_pairs={{0,16},{2,18},{4,20},{6,22},{8,24},{10,26},{12,28},{14,30},{16,0},... | collective-permute-start | bytes 786440 | tf_op jit(solution)/shard_map/ppermute | solution.py:23
  (58 other events, 1042.7 us)
